TPU v7x, 32 devices: a whole 2x2x4 slice. The times are simulated.
32 devices in a mesh: groups: 2 (over y), mem: 4 (over x, core), heads: 4 (over z).
Axes of the slice: x: 2, y: 2, z: 4, core: 2. Of those that a mesh axis runs over, the one named last changes fastest.
Arguments:
- hidden: bfloat16 [32, 8192], P(('groups', 'heads')), parts along dimension 0, may hold values from -6 to 6
- norm_gain: bfloat16 [8192], P('mem'), may hold values from 0.5 to 1.5
- q_weight: bfloat16 [8192, 8192], P('mem', 'heads'), may hold values from -0.0625 to 0.0625
- k_weight: bfloat16 [8192, 1024], P('mem', 'heads'), may hold values from -1 to 1, as said below
- v_weight: bfloat16 [8192, 1024], P('mem', 'heads'), may hold values from -1 to 1, as said below
- o_weight: bfloat16 [8192, 8192], P('heads', 'mem'), may hold values from -0.0625 to 0.0625
- k_cache: bfloat16 [384, 8, 128, 128], P(('groups', 'mem'), 'heads'), parts along dimension 0, may hold values from -40 to 40, as said below
- v_cache: bfloat16 [384, 8, 128, 128], P(('groups', 'mem'), 'heads'), parts along dimension 0, may hold values from -6 to 6, as said below
- page_table: int32 [16, 24], P('groups'), parts along dimension 0, may hold values from 0 to 191, as said below
- attend_list: int32 [16, 8], P('groups'), parts along dimension 0, may hold values from 0 to 23, as said below
- lengths: int32 [16], P('groups'), parts along dimension 0, may hold values from 1409 to 3072, as said below
Outputs:
- layer_out: bfloat16 [32, 8192], P(('groups', 'heads'), 'mem'), parts along dimension 0
There are 2 independent parts, one for each index of `groups`. A program takes and returns all parts, laid end to end along the dimension named above; an argument that names none is the same for every part. Nothing has to cross between parts.
Inputs may be any that keep to these rules, and one draw needn't show every extreme that they name: `page_table`: A permutation of the pool slots 0 to 191 laid out as 8 rows of 24. The blocks named by attend_list lie at most 32 in any one range of slots m * 48 to (m + 1) * 48 - 1, and exactly 32 in some such range. `attend_list`: each row names 8 distinct blocks, all below ceil(lengths[r] / 128), among them its last block ceil(lengths[r] / 128) - 1. `lengths`: some row holds 3072 steps. `k_cache`: each key-value head is stored 1 times, the copies equal. `v_cache`: each key-value head is stored 1 times, the copies equal. `k_weight`: the 1 column blocks of each key-value head are equal. `v_weight`: the 1 column blocks of each key-value head are equal.
All inputs are finite; a program needn't handle non-finite values.
Results may differ from a plain program's by a relative error of at most 0.007.
The roundings to bfloat16 on the way count: a program that leaves them out, or rounds other values in their place, can miss the bound.
Values may be sent and summed in bfloat16 or wider, within the bound.
A program may use at most 64 MiB of HBM per device.

v0:
```python
import jax
import jax.numpy as jnp
from jax import lax
from jax.sharding import PartitionSpec as P

NEG_FILL = -1e30
EPSILON = 1e-05


def fold_owners(running, shard_piece):
    piece_peak, piece_total, piece_accum = shard_piece
    run_peak, run_total, run_accum = running
    joint_peak = jnp.maximum(run_peak, jnp.max(piece_peak, axis=0))
    piece_factor = jnp.exp(piece_peak - joint_peak[None])
    joint_total = jnp.sum(piece_total * piece_factor, axis=0)
    joint_accum = jnp.sum(piece_accum * piece_factor[..., None], axis=0)
    return (joint_peak, joint_total, joint_accum)


def shards(
    hidden,
    norm_gain,
    q_weight,
    k_weight,
    v_weight,
    o_weight,
    k_cache,
    v_cache,
    page_table,
    attend_list,
    lengths,
):
    highest = lax.Precision.HIGHEST
    mem_count = lax.axis_size("mem")
    mem_index = lax.axis_index("mem")
    feature_cols = norm_gain.shape[0]
    hidden_f = hidden.astype(jnp.float32)
    mean_sq = jnp.mean(hidden_f * hidden_f, axis=-1, keepdims=True)
    own_cols = lax.dynamic_slice_in_dim(hidden_f, mem_index * feature_cols, feature_cols, 1)
    normed = (own_cols * lax.rsqrt(mean_sq + EPSILON) * norm_gain.astype(jnp.float32)).astype(
        jnp.bfloat16
    )
    shard_piece = lax.all_gather(normed, "heads", axis=0, tiled=True)
    partial_value = jnp.concatenate(
        [
            jnp.dot(shard_piece, q_weight, preferred_element_type=jnp.float32),
            jnp.dot(shard_piece, k_weight, preferred_element_type=jnp.float32),
            jnp.dot(shard_piece, v_weight, preferred_element_type=jnp.float32),
        ],
        axis=1,
    )
    summed = lax.psum(partial_value, "mem")
    query_cols = q_weight.shape[1]
    value_cols = k_weight.shape[1]
    pool_blocks = k_cache.shape[0]
    local_kv = k_cache.shape[1]
    block_size = k_cache.shape[2]
    head_dim = k_cache.shape[3]
    row_count = lengths.shape[0]
    token_count = summed.shape[0]
    step_count = token_count // row_count
    local_heads = query_cols // head_dim
    per_kv = local_heads // local_kv
    query_count = step_count * per_kv
    scale_factor = head_dim ** (-0.5)
    queries = summed[:, :query_cols].astype(jnp.bfloat16)
    queries = queries.reshape(row_count, step_count, local_kv, per_kv, head_dim).transpose(
        0, 2, 1, 3, 4
    )
    queries = queries.reshape(row_count, local_kv, query_count, head_dim)
    new_keys = summed[:, query_cols : query_cols + value_cols].astype(jnp.bfloat16)
    new_keys = new_keys.reshape(row_count, step_count, local_kv, head_dim).transpose(0, 2, 1, 3)
    new_values = summed[:, query_cols + value_cols :].astype(jnp.bfloat16)
    new_values = new_values.reshape(row_count, step_count, local_kv, head_dim).transpose(0, 2, 1, 3)
    history = page_table.shape[1]
    pair_count = row_count * history
    block_ids = jnp.arange(history, dtype=jnp.int32)
    attended = jnp.any(attend_list[:, :, None] == block_ids[None, None, :], axis=1).reshape(
        pair_count
    )
    slot_global = mem_index * pool_blocks + jnp.arange(pool_blocks, dtype=jnp.int32)
    owner_hit = page_table.reshape(pair_count)[None, :] == slot_global[:, None]
    pair_of_slot = jnp.sum(
        jnp.where(owner_hit, jnp.arange(pair_count, dtype=jnp.int32)[None, :], 0), axis=1
    )
    slot_row = pair_of_slot // history
    slot_block = pair_of_slot % history
    slot_live = jnp.take(attended, pair_of_slot)
    capacity = 2 * row_count * attend_list.shape[1] // mem_count
    running_pos = jnp.cumsum(slot_live.astype(jnp.int32)) - 1
    picked = slot_live[None, :] & (
        running_pos[None, :] == jnp.arange(capacity, dtype=jnp.int32)[:, None]
    )
    chosen = jnp.sum(
        jnp.where(picked, jnp.arange(pool_blocks, dtype=jnp.int32)[None, :], 0), axis=1
    )
    block_keys = jnp.take(k_cache, chosen, axis=0)
    block_values = jnp.take(v_cache, chosen, axis=0)
    block_row = jnp.take(slot_row, chosen)
    block_index = jnp.take(slot_block, chosen)
    block_live = jnp.any(picked, axis=1)
    row_onehot = block_row[:, None] == jnp.arange(row_count, dtype=jnp.int32)[None, :]
    block_queries = jnp.take(queries, block_row, axis=0)
    scores = (
        jnp.einsum("cgqd,cgkd->cgqk", block_queries, block_keys, preferred_element_type=jnp.float32)
        * scale_factor
    )
    positions = block_index[:, None] * block_size + jnp.arange(block_size, dtype=jnp.int32)[None, :]
    valid = (block_live[:, None] & (positions < jnp.take(lengths, block_row)[:, None]))[
        :, None, None, :
    ]
    scores = jnp.where(valid, scores, NEG_FILL)
    block_peak = jnp.max(scores, axis=-1)
    row_peak = jnp.max(
        jnp.where(row_onehot[:, :, None, None], block_peak[:, None], NEG_FILL), axis=0
    )
    weights = jnp.where(
        valid, jnp.exp(scores - jnp.take(row_peak, block_row, axis=0)[..., None]), 0.0
    )
    weights_high = weights.astype(jnp.bfloat16)
    weights_low = (weights - weights_high.astype(jnp.float32)).astype(jnp.bfloat16)
    block_accum = jnp.einsum(
        "cgqk,cgkd->cgqd", weights_high, block_values, preferred_element_type=jnp.float32
    )
    block_accum = block_accum + jnp.einsum(
        "cgqk,cgkd->cgqd", weights_low, block_values, preferred_element_type=jnp.float32
    )
    onehot_f = row_onehot.astype(jnp.float32)
    row_sums = jnp.einsum("cr,cgq->rgq", onehot_f, jnp.sum(weights, axis=-1), precision=highest)
    row_accum = jnp.einsum("cr,cgqd->rgqd", onehot_f, block_accum, precision=highest)
    fresh_scores = (
        jnp.einsum("rgqd,rgtd->rgqt", queries, new_keys, preferred_element_type=jnp.float32)
        * scale_factor
    )
    causal = (
        jnp.arange(step_count, dtype=jnp.int32)[None, :]
        <= (jnp.arange(query_count, dtype=jnp.int32) // per_kv)[:, None]
    )
    fresh_scores = jnp.where(causal, fresh_scores, NEG_FILL)
    start_state = (
        jnp.full_like(row_peak, NEG_FILL),
        jnp.zeros_like(row_sums),
        jnp.zeros_like(row_accum),
    )
    cache_peak, cache_sum, cache_accum = fold_owners(
        start_state,
        (
            lax.all_gather(row_peak[None], "mem", axis=0, tiled=True),
            lax.all_gather(row_sums[None], "mem", axis=0, tiled=True),
            lax.all_gather(row_accum[None], "mem", axis=0, tiled=True),
        ),
    )
    final_peak = jnp.maximum(cache_peak, jnp.max(fresh_scores, axis=-1))
    carried = jnp.exp(cache_peak - final_peak)
    fresh_weights = jnp.where(causal, jnp.exp(fresh_scores - final_peak[..., None]), 0.0)
    final_sum = cache_sum * carried + jnp.sum(fresh_weights, axis=-1)
    final_accum = cache_accum * carried[..., None] + jnp.einsum(
        "rgqt,rgtd->rgqd", fresh_weights, new_values.astype(jnp.float32), precision=highest
    )
    attended_out = (final_accum / final_sum[..., None]).astype(jnp.bfloat16)
    attended_out = attended_out.reshape(
        row_count, local_kv, step_count, per_kv, head_dim
    ).transpose(0, 2, 1, 3, 4)
    attended_out = attended_out.reshape(token_count, query_cols)
    projected = lax.psum_scatter(
        jnp.dot(attended_out, o_weight, preferred_element_type=jnp.float32),
        "heads",
        scatter_dimension=0,
        tiled=True,
    )
    return projected.astype(jnp.bfloat16)


def solution(mesh):
    in_specs = (
        P(("groups", "heads"), None),
        P("mem"),
        P("mem", "heads"),
        P("mem", "heads"),
        P("mem", "heads"),
        P("heads", "mem"),
        P(("groups", "mem"), "heads", None, None),
        P(("groups", "mem"), "heads", None, None),
        P("groups", None),
        P("groups", None),
        P("groups"),
    )
    out_specs = P(("groups", "heads"), "mem")
    return jax.shard_map(shards, mesh=mesh, in_specs=in_specs, out_specs=out_specs, check_vma=False)
```

profile of v0, /device:TPU:0, one launch (start us, length us, event | category | flops | bytes accessed | tf_op | source)
XLA Modules:
  0.0 102.8 jit_solution(13370720556598059067)
XLA Ops:
  0.0 0.9 eq.60
  0.9 0.2 select_reduce_fusion.1
  1.2 0.8 fusion.34
  1.9 0.1 reshape.240
  2.0 0.8 gather_fusion
  2.8 0.1 copy.67
  2.9 0.1 reduce-window.8
  3.0 0.1 add_reduce_fusion
  3.1 0.1 select_reduce_fusion.2
  3.3 0.7 gather_fusion.5
  4.0 0.7 gather_fusion.4
  4.7 0.7 gather_fusion.1
  5.4 0.1 fusion.37
  5.6 0.1 fusion.38
  5.6 0.0 copy-done.6
  5.7 0.2 multiply_reduce_fusion
  5.9 0.1 fusion.35
  6.0 14.9 %all-gather.3 = bf16[4,4,2048]{2,1,0:T(4,128)(2,1)S(1)} all-gather(bf16[1,4,2048]{2,1,0:T(4,128)(2,1)S(1)} %fusion.35), channel_id=1, replica_groups=mesh['groups'=2,'mem'=4,'heads'=4] {'heads'}, dimensions={0}, use_global_device_ids=true | all-gather | bytes 81920 | tf_op jit(solution)/shard_map/all_gather | solution.py:43
  20.9 0.0 copy-start.3
  21.0 4.7 %fusion.62 = f32[16,2048]{1,0:T(8,128)S(1)} fusion(bf16[16,2048]{1,0:T(8,128)(2,1)S(1)} %reshape.322, bf16[2048,2048]{1,0:T(8,128)(2,1)} %param.17), kind=kOutput, calls=%fused_computation.117 | convolution fusion | flops 134217728 | bytes 8585216 | tf_op jit(solution)/shard_map/dot_general | solution.py:46
  25.7 0.3 fusion.63
  25.9 0.3 fusion.64
  26.2 11.7 %all-reduce.3 = bf16[16,2560]{1,0:T(8,128)(2,1)S(1)} all-reduce(f32[16,2560]{1,0:T(8,128)S(1)} %pad_maximum_fusion), channel_id=1, replica_groups=mesh['groups'=2,'mem'=4,'heads'=4] {'mem'}, use_global_device_ids=true, to_apply=%region_6.8 | all-reduce | flops 40960 | bytes 245760 | tf_op jit(solution)/shard_map/psum | solution.py:52
  38.0 1.3 %gather_fusion.2 = bf16[32,2,16,128]{3,2,1,0:T(8,128)(2,1)} fusion(bf16[8,2,16,128]{3,2,1,0:T(8,128)(2,1)S(1)} %bitcast.67, s32[1024]{0:T(1024)S(1)} %pad_clamp_fusion), kind=kCustom, calls=%fused_computation.6 | custom fusion | bytes 524416 | tf_op jit(solution)/shard_map/jit(_take)/gather | solution.py:103
  39.3 2.2 %gather_fusion.6 = bf16[32,2,128,128]{3,2,1,0:T(8,128)(2,1)} fusion(bf16[48,2,128,128]{3,2,1,0:T(8,128)(2,1)S(1)} %copy-done, s32[1024]{0:T(1024)S(1)} %pad_clamp_fusion.1), kind=kCustom, calls=%fused_computation.1.clone | custom fusion | bytes 4194432 | tf_op jit(solution)/shard_map/jit(_take)/gather | solution.py:97
  41.4 3.8 %fusion.60 = (f32[32,2,16]{2,1,0:T(2,128)S(1)}, f32[32,2,16,128]{3,2,1,0:T(8,128)}) fusion(bf16[32,2,128,128]{3,2,1,0:T(8,128)(2,1)} %gather_fusion.6, pred[32]{0:T(512)(128)(4,1)S(1)} %get-tuple-element.12, bf16[32,2,16,128]{3,2,1,0:T(8,128)(2,1)} %gather_fusion.2, pred[32]{0:T(512)(128)(4,1)S(1)} %get-tuple-element.14, pred[32,128]{1,0:T(8,128)(4,1)S(1)} %fusion.38), kind=kOutput, calls=%fused_computation.115 | convolution fusion | flops 35126272 | bytes 2891840 | tf_op jit(solution)/shard_map/cgqd,cgkd->cgqk/dot_general | solution.py:105
  45.2 0.1 copy.69
  45.3 0.1 select_reduce_fusion
  45.4 5.3 %all-gather.1 = f32[32,2,16]{2,1,0:T(2,128)S(1)} all-gather(f32[8,2,16]{2,1,0:T(2,128)S(1)} %select_reduce_fusion), channel_id=3, replica_groups=mesh['groups'=2,'mem'=4,'heads'=4] {'mem'}, dimensions={0}, use_global_device_ids=true | all-gather | bytes 5120 | tf_op jit(solution)/shard_map/all_gather | solution.py:148
  50.8 0.2 fusion.61
  51.1 0.6 gather_fusion.3
  51.7 0.1 broadcast_select_fusion.3
  51.8 1.4 %fusion.18 = f32[32,2,16]{2,1,0:T(2,128)S(1)} fusion(f32[32,2,16,128]{3,2,1,0:T(8,128)} %get-tuple-element.24, f32[32,2,16]{2,1,0:T(2,128)S(1)} %broadcast_select_fusion.3, pred[32,128]{1,0:T(8,128)(4,1)S(1)} %fusion.38), kind=kLoop, calls=%fused_computation.29 | loop fusion | flops 392192 | bytes 536576 | tf_op jit(solution)/shard_map/reduce_sum | solution.py:129
  53.3 0.1 fusion.31
  53.4 5.4 %all-gather.2 = f32[32,2,16]{2,0,1:T(8,128)S(1)} all-gather(f32[8,2,16]{2,0,1:T(8,128)S(1)} %fusion.31), channel_id=4, replica_groups=mesh['groups'=2,'mem'=4,'heads'=4] {'mem'}, dimensions={0}, use_global_device_ids=true | all-gather | bytes 5120 | tf_op jit(solution)/shard_map/all_gather | solution.py:149
  58.9 0.1 copy.73
  59.0 4.1 %gather_fusion.7 = bf16[32,2,128,128]{3,2,1,0:T(8,128)(2,1)} fusion(bf16[48,2,128,128]{3,2,1,0:T(8,128)(2,1)} %param.22, s32[1024]{0:T(1024)S(1)} %pad_clamp_fusion.1), kind=kCustom, calls=%fused_computation.3.clone | custom fusion | bytes 4194432 | tf_op jit(solution)/shard_map/jit(_take)/gather | solution.py:98
  63.0 2.6 %fusion.14 = f32[32,2,16,128]{3,2,1,0:T(8,128)S(1)} fusion(bf16[32,2,128,128]{3,2,1,0:T(8,128)(2,1)} %gather_fusion.7, pred[32]{0:T(512)(128)(4,1)S(1)} %get-tuple-element.12, f32[32,2,16,128]{3,2,1,0:T(8,128)} %get-tuple-element.24, f32[32,2,16]{2,1,0:T(2,128)S(1)} %broadcast_select_fusion.3, pred[32,128]{1,0:T(8,128)(4,1)S(1)} %fusion.38), kind=kOutput, calls=%fused_computation.22 | convolution fusion | flops 34996224 | bytes 3153952 | tf_op jit(solution)/shard_map/cgqk,cgkd->cgqd/dot_general | solution.py:122
  65.6 0.7 convolution_add_fusion
  66.4 0.6 fusion.16
  67.0 7.4 %all-gather = f32[32,2,16,128]{3,0,2,1:T(8,128)S(1)} all-gather(f32[8,2,16,128]{3,0,2,1:T(8,128)S(1)} %fusion.16), channel_id=2, replica_groups=mesh['groups'=2,'mem'=4,'heads'=4] {'mem'}, dimensions={0}, use_global_device_ids=true | all-gather | bytes 655360 | tf_op jit(solution)/shard_map/all_gather | solution.py:150
  74.4 0.2 fusion.15
  74.6 0.3 fusion.11
  75.0 0.0 copy-start.8
  75.0 4.6 %fusion.65 = f32[16,2048]{1,0:T(8,128)S(1)} fusion(bf16[16,2048]{1,0:T(8,128)(2,1)S(1)} %reshape.246, bf16[2048,2048]{1,0:T(8,128)(2,1)} %param.20), kind=kOutput, calls=%fused_computation.120 | convolution fusion | flops 134217728 | bytes 8585216 | tf_op jit(solution)/shard_map/dot_general | solution.py:166
  79.6 21.4 %all-reduce.4 = bf16[16,2048]{1,0:T(8,128)(2,1)S(1)} all-reduce(f32[16,2048]{1,0:T(8,128)S(1)} %fusion.65), channel_id=5, replica_groups=mesh['groups'=2,'mem'=4,'heads'=4] {'heads'}, use_global_device_ids=true, to_apply=%region_15.18.clone | all-reduce | flops 32768 | bytes 196608
  101.0 0.6 dynamic-slice
  102.2 0.6 dynamic-slice_convert_fusion
  (49 shorter events, 0.4 us)
Async XLA Ops:
  0.0 39.3 %copy-start = (bf16[48,2,128,128]{3,2,1,0:T(8,128)(2,1)S(1)}, bf16[48,2,128,128]{3,2,1,0:T(8,128)(2,1)}, u32[]{:S(2)}) copy-start(bf16[48,2,128,128]{3,2,1,0:T(8,128)(2,1)} %param.21) | copy-start | bytes 9437188
  0.0 4.7 %copy-start.1 = (s32[8]{0:T(128)S(1)}, s32[8]{0:T(128)}, u32[]{:S(2)}) copy-start(s32[8]{0:T(128)} %param.25) | copy-start | bytes 100
  0.0 5.6 %copy-start.6 = (bf16[4,8192]{1,0:T(4,128)(2,1)S(1)}, bf16[4,8192]{1,0:T(4,128)(2,1)}, u32[]{:S(2)}) copy-start(bf16[4,8192]{1,0:T(4,128)(2,1)} %param.15) | copy-start | bytes 196612
  0.0 5.7 %copy-start.7 = (bf16[2048]{0:T(1024)(128)(2,1)S(1)}, bf16[2048]{0:T(1024)(128)(2,1)}, u32[]{:S(2)}) copy-start(bf16[2048]{0:T(1024)(128)(2,1)} %param.16) | copy-start | bytes 12292
  20.9 4.7 %copy-start.3 = (bf16[2048,256]{1,0:T(8,128)(2,1)S(1)}, bf16[2048,256]{1,0:T(8,128)(2,1)}, u32[]{:S(2)}) copy-start(bf16[2048,256]{1,0:T(8,128)(2,1)} %param.18) | copy-start | bytes 3145732
  20.9 5.0 %copy-start.4 = (bf16[2048,256]{1,0:T(8,128)(2,1)S(1)}, bf16[2048,256]{1,0:T(8,128)(2,1)}, u32[]{:S(2)}) copy-start(bf16[2048,256]{1,0:T(8,128)(2,1)} %param.19) | copy-start | bytes 3145732
  63.0 2.6 %copy-start.2 = (bf16[32,2,128,128]{3,2,1,0:T(8,128)(2,1)S(1)}, bf16[32,2,128,128]{3,2,1,0:T(8,128)(2,1)}, u32[]{:S(2)}) copy-start(bf16[32,2,128,128]{3,2,1,0:T(8,128)(2,1)} %gather_fusion.7) | copy-start | bytes 6291460
  63.0 2.6 %copy-start.5 = (f32[32,2,16,128]{3,2,1,0:T(8,128)S(1)}, f32[32,2,16,128]{3,2,1,0:T(8,128)}, u32[]{:S(2)}) copy-start(f32[32,2,16,128]{3,2,1,0:T(8,128)} %get-tuple-element.24) | copy-start | bytes 1572868
  75.0 26.0 %copy-start.8 = (u32[32]{0:T(128)S(1)}, u32[32]{0:T(128)}, u32[]{:S(2)}) copy-start(u32[32]{0:T(128)} %constant.151) | copy-start | bytes 388
where the time goes:
time: 103 us
  blocking collectives  66.2 us (64%)
  matrix products  18.2 us (18%)
  local copies, waits for them, and re-layouts  13.6 us (13%)
  other arithmetic  3.86 us (4%)
    unnamed x1, blocking collectives  21.4 us
    all_gather x1, blocking collectives, shards(): shard_piece = lax.all_gather(normed, 'heads', axis=0, tiled=True)  14.9 us
    psum x1, blocking collectives, shards(): summed = lax.psum(partial_value, 'mem')  11.7 us
    all_gather x1, blocking collectives, shards(): lax.all_gather(row_accum[None], 'mem', axis=0, tiled=True)  7.38 us
    all_gather x1, blocking collectives, shards(): lax.all_gather(row_sums[None], 'mem', axis=0, tiled=True)  5.43 us
    all_gather x1, blocking collectives, shards(): lax.all_gather(row_peak[None], 'mem', axis=0, tiled=True)  5.32 us
    dot_general x1, matrix products, shards(): jnp.dot(shard_piece, q_weight, preferred_element_type=jnp.float32)  4.72 us
    dot_general x1, matrix products, shards(): jnp.dot(attended_out, o_weight, preferred_element_type=jnp.float32)  4.58 us

commit v1 on v0

--- a/solution.py
+++ b/solution.py
@@ -40,7 +40,14 @@
     normed = (own_cols * lax.rsqrt(mean_sq + EPSILON) * norm_gain.astype(jnp.float32)).astype(
         jnp.bfloat16
     )
-    shard_piece = lax.all_gather(normed, "heads", axis=0, tiled=True)
+    ring = [normed]
+    for hop in range(3):
+        ring.append(lax.ppermute(ring[-1], "heads", [(dev, (dev + 1) % 4) for dev in range(4)]))
+    shard_piece = jnp.roll(
+        jnp.concatenate(ring[::-1], axis=0),
+        (lax.axis_index("heads") + 1) * ring[0].shape[0],
+        axis=0,
+    )
     partial_value = jnp.concatenate(
         [
             jnp.dot(shard_piece, q_weight, preferred_element_type=jnp.float32),

time: 103 us -> 105 us (1.019)
  blocking collectives: 66.2 us -> 52 us
  other arithmetic: 3.86 us -> 10.3 us
  starting transfers between devices: 0 us -> 4.68 us
  waiting for transfers between devices: 0 us -> 3.96 us
  matrix products: 18.2 us -> 19.3 us
    all_gather x1 -> x0, blocking collectives: 14.9 us -> none  [shards(): shard_piece = lax.all_gather(normed, 'heads', axis=0, tiled=True)]
    ppermute x0 -> x3, starting transfers between devices: none -> 4.68 us  [shards(): lax.ppermute(ring[-1], 'heads', [(dev, (dev + 1) % 4) for dev in range(4)])]
    ppermute x0 -> x3, waiting for transfers between devices: none -> 3.96 us  [shards(): lax.ppermute(ring[-1], 'heads', [(dev, (dev + 1) % 4) for dev in range(4)])]
    reduce_sum x1, other arithmetic: 0.2 us -> 1.25 us  [fold_owners(): joint_accum = jnp.sum(piece_accum * piece_factor[..., None], axis=0)]
  transfers between devices with their start and end apart: 0 -> 3, of which waited for: 0 -> 1; matrix products, arithmetic and copies ran while one was open for 0% -> 14% of each run, Pallas kernels for 0% -> 0%
where the time goes in v1:
time: 105 us; the launch traced here: 104 us
  blocking collectives  52 us (50%)
  matrix products  19.3 us (18%)
  local copies, waits for them, and re-layouts  13.1 us (12%)
  other arithmetic  10.3 us (10%)
  starting transfers between devices  4.68 us (4%)
  waiting for transfers between devices  3.96 us (4%)
    unnamed x1, blocking collectives  21.7 us
    psum x1, blocking collectives, shards(): summed = lax.psum(partial_value, 'mem')  11.7 us
    all_gather x1, blocking collectives, shards(): lax.all_gather(row_accum[None], 'mem', axis=0, tiled=True)  7.83 us
    all_gather x1, blocking collectives, shards(): lax.all_gather(row_sums[None], 'mem', axis=0, tiled=True)  5.43 us
    all_gather x1, blocking collectives, shards(): lax.all_gather(row_peak[None], 'mem', axis=0, tiled=True)  5.32 us
    dot_general x1, matrix products, shards(): jnp.dot(shard_piece, q_weight, preferred_element_type=jnp.float32)  4.73 us
    ppermute x3, starting transfers between devices, shards(): lax.ppermute(ring[-1], 'heads', [(dev, (dev + 1) % 4) for dev in range(4)])  4.68 us
    dot_general x1, matrix products, shards(): jnp.dot(attended_out, o_weight, preferred_element_type=jnp.float32)  4.58 us
  transfers between devices with their start and end apart: 3, of which 1 were waited for; matrix products, arithmetic and copies ran while one was open for 14% of the time, Pallas kernels for 0%

profile of v1, /device:TPU:0, one launch (start us, length us, event | category | flops | bytes accessed | tf_op | source)
XLA Modules:
  0.0 104.4 jit_solution(16197226178615395177)
XLA Ops:
  0.0 1.0 convert_element_type.42
  1.0 1.0 multiply_reduce_fusion
  2.0 0.7 convert_element_type.43
  2.8 3.1 %collective-permute-start = (bf16[4,2048]{1,0:T(4,128)(2,1)S(1)}, bf16[4,2048]{1,0:T(4,128)(2,1)S(1)}, u32[]{:S(2)}, u32[]{:S(2)}) collective-permute-start(bf16[4,2048]{1,0:T(4,128)(2,1)S(1)} %multiply_convert_fusion), channel_id=1, source_target_pairs={{0,1},{1,2},{2,3},{3,0},{4,5},{5,6},{6,7},{7,4},{8,9},{9,10},{10,1... | collective-permute-start | bytes 49160 | tf_op jit(solution)/shard_map/ppermute | solution.py:45
  5.9 0.8 eq.63
  6.7 0.2 select_reduce_fusion.1
  6.9 0.8 fusion.40
  7.8 0.8 gather_fusion
  8.6 0.1 copy.67
  8.8 0.1 add_reduce_fusion
  8.9 0.1 select_reduce_fusion.2
  9.0 0.1 fusion.42
  9.2 0.7 gather_fusion.5
  9.9 0.7 gather_fusion.4
  10.6 0.7 gather_fusion.1
  11.3 0.5 broadcast_select_fusion.4
  11.9 0.7 fusion.43
  12.5 0.6 iota_compare_fusion.2
  13.1 1.6 %collective-permute-start.1 = (bf16[4,2048]{1,0:T(4,128)(2,1)S(1)}, bf16[4,2048]{1,0:T(4,128)(2,1)S(1)}, u32[]{:S(2)}, u32[]{:S(2)}) collective-permute-start(bf16[4,2048]{1,0:T(4,128)(2,1)S(1)} %collective-permute-done), channel_id=1, source_target_pairs={{0,1},{1,2},{2,3},{3,0},{4,5},{5,6},{6,7},{7,4},{8,9},{9,10},{10,1... | collective-permute-start | bytes 49160 | tf_op jit(solution)/shard_map/ppermute | solution.py:45
  14.7 4.0 %collective-permute-done.1 = bf16[4,2048]{1,0:T(4,128)(2,1)S(1)} collective-permute-done((bf16[4,2048]{1,0:T(4,128)(2,1)S(1)}, bf16[4,2048]{1,0:T(4,128)(2,1)S(1)}, u32[]{:S(2)}, u32[]{:S(2)}) %collective-permute-start.1) | collective-permute-done | bytes 16416 | tf_op jit(solution)/shard_map/ppermute | solution.py:45
  18.7 0.6 iota_compare_fusion.5
  19.2 2.1 %gather_fusion.6 = bf16[32,2,128,128]{3,2,1,0:T(8,128)(2,1)} fusion(bf16[48,2,128,128]{3,2,1,0:T(8,128)(2,1)S(1)} %copy-done, s32[1024]{0:T(1024)S(1)} %pad_clamp_fusion.1), kind=kCustom, calls=%fused_computation.1.clone | custom fusion | bytes 4194432 | tf_op jit(solution)/shard_map/jit(_take)/gather | solution.py:104
  21.4 4.1 %gather_fusion.7 = bf16[32,2,128,128]{3,2,1,0:T(8,128)(2,1)} fusion(bf16[48,2,128,128]{3,2,1,0:T(8,128)(2,1)} %param.22, s32[1024]{0:T(1024)S(1)} %pad_clamp_fusion.1), kind=kCustom, calls=%fused_computation.3.clone | custom fusion | bytes 4194432 | tf_op jit(solution)/shard_map/jit(_take)/gather | solution.py:105
  25.4 0.6 dynamic-slice
  26.6 0.1 concatenate.9
  26.8 4.7 %fusion.34 = f32[16,2048]{1,0:T(8,128)S(1)} fusion(bf16[2048,2048]{1,0:T(8,128)(2,1)} %param.17, bf16[32,2048]{1,0:T(8,128)(2,1)S(1)} %concatenate.9, s32[]{:T(128)S(6)} %select_n.160), kind=kOutput, calls=%fused_computation.51 | convolution fusion | flops 134217728 | bytes 8585220 | tf_op jit(solution)/shard_map/dot_general | solution.py:53
  31.5 0.3 fusion.30
  31.8 0.3 fusion.32
  32.1 11.7 %all-reduce.3 = bf16[16,2560]{1,0:T(8,128)(2,1)S(1)} all-reduce(f32[16,2560]{1,0:T(8,128)S(1)} %pad_maximum_fusion), channel_id=1, replica_groups=mesh['groups'=2,'mem'=4,'heads'=4] {'mem'}, use_global_device_ids=true, to_apply=%region_6.8 | all-reduce | flops 40960 | bytes 245760 | tf_op jit(solution)/shard_map/psum | solution.py:59
  43.9 0.7 gather_fusion.2
  44.6 3.7 %fusion.68 = (f32[32,2,16]{2,1,0:T(2,128)S(1)}, f32[32,2,16,128]{3,2,1,0:T(8,128)}) fusion(bf16[32,2,128,128]{3,2,1,0:T(8,128)(2,1)} %gather_fusion.6, pred[32]{0:T(512)(128)(4,1)} %copy-done.10, bf16[32,2,16,128]{3,2,1,0:T(8,128)(2,1)S(1)} %gather_fusion.2, pred[32]{0:T(512)(128)(4,1)} %get-tuple-element.14, pred[32,128]{1,0:T(8,128)(4,1)} %fusion.43), kind=kOutput, calls=%fused_computation.123 | convolution fusion | flops 35126272 | bytes 2891840 | tf_op jit(solution)/shard_map/cgqd,cgkd->cgqk/dot_general | solution.py:112
  48.4 0.1 select_reduce_fusion
  48.5 5.3 %all-gather.1 = f32[32,2,16]{2,1,0:T(2,128)S(1)} all-gather(f32[8,2,16]{2,1,0:T(2,128)S(1)} %select_reduce_fusion), channel_id=3, replica_groups=mesh['groups'=2,'mem'=4,'heads'=4] {'mem'}, dimensions={0}, use_global_device_ids=true | all-gather | bytes 5120 | tf_op jit(solution)/shard_map/all_gather | solution.py:155
  53.8 0.7 gather_fusion.3
  54.6 0.8 fusion.69
  55.4 0.7 broadcast_select_fusion.3
  56.2 1.4 %fusion.18 = f32[32,2,16]{2,1,0:T(2,128)S(1)} fusion(f32[32,2,16,128]{3,2,1,0:T(8,128)} %get-tuple-element.24, f32[32,2,16]{2,1,0:T(2,128)S(1)} %broadcast_select_fusion.3, pred[32,128]{1,0:T(8,128)(4,1)} %fusion.43), kind=kLoop, calls=%fused_computation.29 | loop fusion | flops 392192 | bytes 536576 | tf_op jit(solution)/shard_map/reduce_sum | solution.py:136
  57.6 0.7 fusion.37
  58.3 5.4 %all-gather.2 = f32[32,2,16]{2,0,1:T(8,128)S(1)} all-gather(f32[8,2,16]{2,0,1:T(8,128)S(1)} %fusion.37), channel_id=4, replica_groups=mesh['groups'=2,'mem'=4,'heads'=4] {'mem'}, dimensions={0}, use_global_device_ids=true | all-gather | bytes 5120 | tf_op jit(solution)/shard_map/all_gather | solution.py:156
  63.9 2.6 %fusion.14 = f32[32,2,16,128]{3,2,1,0:T(8,128)S(1)} fusion(bf16[32,2,128,128]{3,2,1,0:T(8,128)(2,1)} %gather_fusion.7, pred[32]{0:T(512)(128)(4,1)} %copy-done.10, f32[32,2,16,128]{3,2,1,0:T(8,128)} %get-tuple-element.24, f32[32,2,16]{2,1,0:T(2,128)S(1)} %broadcast_select_fusion.3, pred[32,128]{1,0:T(8,128)(4,1)} %fusion.43), kind=kOutput, calls=%fused_computation.22 | convolution fusion | flops 34996224 | bytes 3153952 | tf_op jit(solution)/shard_map/cgqk,cgkd->cgqd/dot_general | solution.py:129
  66.6 0.7 convolution_add_fusion
  67.3 0.6 fusion.16
  67.9 7.8 %all-gather = f32[32,2,16,128]{3,0,2,1:T(8,128)} all-gather(f32[8,2,16,128]{3,0,2,1:T(8,128)S(1)} %fusion.16), channel_id=2, replica_groups=mesh['groups'=2,'mem'=4,'heads'=4] {'mem'}, dimensions={0}, use_global_device_ids=true | all-gather | bytes 655360 | tf_op jit(solution)/shard_map/all_gather | solution.py:157
  75.8 1.3 %fusion.15 = f32[8,2,16,128]{3,0,2,1:T(8,128)S(1)} fusion(f32[32,2,16,128]{3,0,2,1:T(8,128)} %all-gather, f32[4,8,2,16]{1,0,3,2:T(4,128)S(1)} %copy.73), kind=kLoop, calls=%fused_computation.24 | loop fusion | flops 229376 | bytes 659456 | tf_op jit(solution)/shard_map/reduce_sum | solution.py:16
  77.1 0.3 fusion.11
  77.5 4.6 %fusion.70 = f32[16,2048]{1,0:T(8,128)S(1)} fusion(bf16[16,2048]{1,0:T(8,128)(2,1)S(1)} %reshape.246, bf16[2048,2048]{1,0:T(8,128)(2,1)} %param.20), kind=kOutput, calls=%fused_computation.125 | convolution fusion | flops 134217728 | bytes 8585216 | tf_op jit(solution)/shard_map/dot_general | solution.py:173
  82.1 21.7 %all-reduce.4 = bf16[16,2048]{1,0:T(8,128)(2,1)S(1)} all-reduce(f32[16,2048]{1,0:T(8,128)S(1)} %fusion.70), channel_id=5, replica_groups=mesh['groups'=2,'mem'=4,'heads'=4] {'heads'}, use_global_device_ids=true, to_apply=%region_15.18.clone | all-reduce | flops 32768 | bytes 196608
  103.8 0.6 dynamic-slice_convert_fusion
  (66 shorter events, 0.8 us)
Async XLA Ops:
  0.0 19.2 %copy-start = (bf16[48,2,128,128]{3,2,1,0:T(8,128)(2,1)S(1)}, bf16[48,2,128,128]{3,2,1,0:T(8,128)(2,1)}, u32[]{:S(2)}) copy-start(bf16[48,2,128,128]{3,2,1,0:T(8,128)(2,1)} %param.21) | copy-start | bytes 9437188
  0.0 10.6 %copy-start.1 = (s32[8]{0:T(128)S(1)}, s32[8]{0:T(128)}, u32[]{:S(2)}) copy-start(s32[8]{0:T(128)} %param.25) | copy-start | bytes 100
  2.8 10.3 %collective-permute-start = (bf16[4,2048]{1,0:T(4,128)(2,1)S(1)}, bf16[4,2048]{1,0:T(4,128)(2,1)S(1)}, u32[]{:S(2)}, u32[]{:S(2)}) collective-permute-start(bf16[4,2048]{1,0:T(4,128)(2,1)S(1)} %multiply_convert_fusion), channel_id=1, source_target_pairs={{0,1},{1,2},{2,3},{3,0},{4,5},{5,6},{6,7},{7,4},{8,9},{9,10},{10,1... | collective-permute-start | bytes 49160 | tf_op jit(solution)/shard_map/ppermute | solution.py:45
  9.9 0.7 copy-start.10
  10.6 10.8 %copy-start.7 = (s32[32]{0:T(128)}, s32[32]{0:T(128)S(1)}, u32[]{:S(2)}) copy-start(s32[32]{0:T(128)S(1)} %get-tuple-element.16) | copy-start | bytes 388
  10.6 10.7 %copy-start.9 = (s32[1024]{0:T(1024)}, s32[1024]{0:T(1024)S(1)}, u32[]{:S(2)}) copy-start(s32[1024]{0:T(1024)S(1)} %pad_clamp_fusion) | copy-start | bytes 12292
  13.1 5.5 %collective-permute-start.1 = (bf16[4,2048]{1,0:T(4,128)(2,1)S(1)}, bf16[4,2048]{1,0:T(4,128)(2,1)S(1)}, u32[]{:S(2)}, u32[]{:S(2)}) collective-permute-start(bf16[4,2048]{1,0:T(4,128)(2,1)S(1)} %collective-permute-done), channel_id=1, source_target_pairs={{0,1},{1,2},{2,3},{3,0},{4,5},{5,6},{6,7},{7,4},{8,9},{9,10},{10,1... | collective-permute-start | bytes 49160 | tf_op jit(solution)/shard_map/ppermute | solution.py:45
  18.7 8.0 %collective-permute-start.2 = (bf16[4,2048]{1,0:T(4,128)(2,1)S(1)}, bf16[4,2048]{1,0:T(4,128)(2,1)S(1)}, u32[]{:S(2)}, u32[]{:S(2)}) collective-permute-start(bf16[4,2048]{1,0:T(4,128)(2,1)S(1)} %collective-permute-done.1), channel_id=1, source_target_pairs={{0,1},{1,2},{2,3},{3,0},{4,5},{5,6},{6,7},{7,4},{8,9},{9,10},{10,1... | collective-permute-start | bytes 49160 | tf_op jit(solution)/shard_map/ppermute | solution.py:45
  21.3 4.1 %copy-start.14 = (u32[32]{0:T(128)S(1)}, u32[32]{0:T(128)}, u32[]{:S(2)}) copy-start(u32[32]{0:T(128)} %constant.176) | copy-start | bytes 388
  26.8 4.8 %copy-start.3 = (bf16[2048,256]{1,0:T(8,128)(2,1)S(1)}, bf16[2048,256]{1,0:T(8,128)(2,1)}, u32[]{:S(2)}) copy-start(bf16[2048,256]{1,0:T(8,128)(2,1)} %param.19) | copy-start | bytes 3145732
  26.8 5.0 %copy-start.4 = (bf16[2048,256]{1,0:T(8,128)(2,1)S(1)}, bf16[2048,256]{1,0:T(8,128)(2,1)}, u32[]{:S(2)}) copy-start(bf16[2048,256]{1,0:T(8,128)(2,1)} %param.18) | copy-start | bytes 3145732
  44.6 3.8 %copy-start.12 = (pred[32,8]{0,1:T(8,128)(4,1)S(1)}, pred[32,8]{0,1:T(8,128)(4,1)}, u32[]{:S(2)}) copy-start(pred[32,8]{0,1:T(8,128)(4,1)} %iota_compare_fusion.2) | copy-start | bytes 772
  63.9 2.7 %copy-start.2 = (bf16[32,2,128,128]{3,2,1,0:T(8,128)(2,1)S(1)}, bf16[32,2,128,128]{3,2,1,0:T(8,128)(2,1)}, u32[]{:S(2)}) copy-start(bf16[32,2,128,128]{3,2,1,0:T(8,128)(2,1)} %gather_fusion.7) | copy-start | bytes 6291460
  63.9 2.7 %copy-start.5 = (f32[32,2,16,128]{3,2,1,0:T(8,128)S(1)}, f32[32,2,16,128]{3,2,1,0:T(8,128)}, u32[]{:S(2)}) copy-start(f32[32,2,16,128]{3,2,1,0:T(8,128)} %get-tuple-element.24) | copy-start | bytes 1572868
  63.9 2.7 %copy-start.6 = (pred[32,128]{1,0:T(8,128)(4,1)S(1)}, pred[32,128]{1,0:T(8,128)(4,1)}, u32[]{:S(2)}) copy-start(pred[32,128]{1,0:T(8,128)(4,1)} %fusion.43) | copy-start | bytes 12292
  63.9 2.7 %copy-start.11 = (pred[32]{0:T(512)(128)(4,1)S(1)}, pred[32]{0:T(512)(128)(4,1)}, u32[]{:S(2)}) copy-start(pred[32]{0:T(512)(128)(4,1)} %copy-done.10) | copy-start | bytes 100
  66.6 0.8 copy-start.8
  66.6 9.2 %copy-start.13 = (pred[16,2]{0,1:T(4,128)(4,1)S(1)}, pred[16,2]{0,1:T(4,128)(4,1)}, u32[]{:S(2)}) copy-start(pred[16,2]{0,1:T(4,128)(4,1)} %iota_compare_fusion.5) | copy-start | bytes 100
